TPU v7x, 128 devices: a whole 4x4x4 slice. The times are simulated.
128 devices in a mesh: wide: 8 (over y, core), sixteen: 16 (over z, x).
Axes of the slice: x: 4, y: 4, z: 4, core: 2. Of those that a mesh axis runs over, the one named last changes fastest.
Arguments:
- observations: float32 [64, 512, 1024], P(None, 'sixteen', 'wide'), may hold values from -60 to 60
- huber_scale: float32 [64], replicated, may hold values from 0.5 to 2
- observed: int32 [512, 1024], P('sixteen', 'wide'), may hold values from 0 to 1, as said below
- jitter: float32 [2, 512, 1024], P(None, 'sixteen', 'wide'), may hold values from -0.4 to 0.4
- owner_map: int32 [8, 128], P('wide'), may hold values from 0 to 15, as said below
- neighbours: int32 [8, 128, 6], P('wide'), may hold values from 0 to 127, as said below
Outputs:
- solution: float32 [8, 16, 64, 8, 512], P('wide', 'sixteen')
- residual: float32 [8, 16, 64, 8, 512], P('wide', 'sixteen')
Inputs may be any that keep to these rules, and one draw needn't show every extreme that they name: At least one whole lattice row and at least one whole lattice column hold no observed point. `owner_map`: in each column group every device along sixteen holds 8 blocks (block g on device g // 8) and sends them to 8 different owners; every owner receives exactly 8 blocks, each from a different device. `neighbours`: block g of a column group lists g + d and g - d modulo 128 for each of half of 6 different offsets d between 1 and 4; all blocks of one group use the same offsets, so every list holds 6 different blocks and the relation is symmetric.
All inputs are finite; a program needn't handle non-finite values.
Results may differ from a plain program's by a relative error of at most 0.0003.
Values sent between devices are 32-bit elements; how exact they have to be, the bound alone decides.
No kernel may reach another device: no remote copies, remote signals or barrier semaphores. Data moves between devices by JAX's collectives and lax.ppermute only.
A program may use at most 192 MiB of HBM per device.

v0:
```python
import functools

import jax
import jax.numpy as jnp
from jax import lax
from jax.sharding import Mesh
from jax.sharding import PartitionSpec as P

BLOCK = 512
BLOCKS_DEV = 8
REACH = 4
NEIGHBOURS = 6
SWEEPS = 2
ITERS = 2
WIDE = ("wide_0", "wide_1")
SIXTEEN = ("sixteen_0", "sixteen_1")
WIDE_SIXTEEN = ("wide_0", "wide_1", "sixteen_0", "sixteen_1")


HUBER_EDGE = 1.345
NUGGET_TERM = 1.0
SILL_TERM = 0.02
ROOT_THREE = 1.7320508075688772
EXACT = lax.Precision.HIGHEST


def sent_to_all(shard, axis):
    peers = lax.axis_size(axis)
    return lax.all_to_all(
        jnp.broadcast_to(shard[None], (peers, *shard.shape)), axis, 0, 0, tiled=True
    )


def over_copies(shard, axis):
    everything = sent_to_all(shard, axis)
    return jnp.sum(everything, axis=0)


def padded(shard, sides, width):
    for axis, dim in sides:
        peers, length = (lax.axis_size(axis), shard.shape[dim])
        up = [(i, (i + 1) % peers) for i in range(peers)]
        down = [(j, i) for i, j in up]
        last = lax.slice_in_dim(shard, length - width, length, axis=dim)
        initial = lax.slice_in_dim(shard, 0, width, axis=dim)
        before = lax.ppermute(last, axis, up)
        after = lax.ppermute(initial, axis, down)
        shard = jnp.concatenate([before, shard, after], axis=dim)
    return shard


def one_axis_at_a_time(shard, axes):
    return functools.reduce(lax.psum, axes, shard)


def split_up(shard, dim, peers):
    dims = shard.shape
    pieces = shard.reshape(*dims[:dim], peers, dims[dim] // peers, *dims[dim + 1 :])
    return jnp.moveaxis(pieces, dim, 0)


def edges_of(length, count):
    unit = 8 if length >= 8 * count else 1
    return [length // unit * k // count * unit for k in range(1, count)]


def in_order(pieces, dim):
    pieces = jnp.moveaxis(pieces, 0, dim)
    dims = pieces.shape
    return pieces.reshape(*dims[:dim], dims[dim] * dims[dim + 1], *dims[dim + 2 :])


def exchange_in_pieces(shard, axis, pieces, split_dim, concat_dim):
    blocks = split_up(shard, split_dim, lax.axis_size(axis))
    cut = max(range(1, max(2, blocks.ndim - 1)), key=lambda d: blocks.shape[d])
    outs = []
    for section in jnp.split(blocks, edges_of(blocks.shape[cut], pieces), axis=cut):
        if section.size:
            outs.append(lax.all_to_all(section, axis, split_axis=0, concat_axis=0, tiled=True))
    return in_order(jnp.concatenate(outs, axis=cut), concat_dim)


def covariance(centre, others, strip_rows):
    spread = 2.0 * strip_rows
    cutoff = 6.0 * strip_rows
    row_gap = others[0][:, :, None] - centre[0][None, None, :]
    col_gap = others[1][:, :, None] - centre[1][None, None, :]
    distance = jnp.sqrt(row_gap * row_gap + col_gap * col_gap)
    scaled = ROOT_THREE * distance / spread
    fading = jnp.maximum(1.0 - distance / cutoff, 0.0)
    return (
        SILL_TERM * (1.0 + scaled) * jnp.exp(-scaled) * fading**4 * (1.0 + 4.0 * distance / cutoff)
    )


def owned_table(group_map, owners, per_owner):
    total_strips = group_map.shape[0]
    member = (group_map[None, :] == jnp.arange(owners, dtype=jnp.int32)[:, None]).astype(jnp.int32)
    ranked = jnp.cumsum(member, axis=1, dtype=jnp.int32) - 1
    slot_hit = (ranked[:, :, None] == jnp.arange(per_owner, dtype=jnp.int32)[None, None, :]).astype(
        jnp.int32
    ) * member[:, :, None]
    numbers = jnp.arange(total_strips, dtype=jnp.int32)
    return jnp.sum(slot_hit * numbers[None, :, None], axis=1, dtype=jnp.int32)


def outgoing(observed_values, targets, owners):
    chooser = (targets[:, None] == jnp.arange(owners, dtype=jnp.int32)[None, :]).astype(jnp.float32)
    return jnp.einsum("ckb,ko->cob", observed_values, chooser, precision=EXACT)


def incoming(observed_values, owned_ids, per_owner):
    sources = observed_values.shape[1]
    chooser = (
        owned_ids[:, None] // per_owner == jnp.arange(sources, dtype=jnp.int32)[None, :]
    ).astype(jnp.float32)
    return jnp.einsum("csb,js->cjb", observed_values, chooser, precision=EXACT)


def sum_rows(observed_values):
    return jax.tree.map(lambda part: over_copies(part, WIDE), observed_values)


def sum_columns(observed_values):
    return jax.tree.map(lambda part: over_copies(part, SIXTEEN), observed_values)


def on_device(observations, huber_scale, observed, jitter, owner_map, neighbours):
    fields, row_dev, col_dev = observations.shape
    sixteen_size = lax.axis_size(SIXTEEN)
    my_place = lax.axis_index(SIXTEEN)
    group_place = lax.axis_index(WIDE)
    strip_rows = BLOCK // col_dev
    total_strips = BLOCKS_DEV * sixteen_size
    block_numbers = jnp.arange(BLOCKS_DEV, dtype=jnp.int32)
    weight = observed.astype(jnp.float32)
    spread_scale = huber_scale[:, None, None]
    row_effect = jnp.zeros((fields, row_dev), jnp.float32)
    col_effect = jnp.zeros((fields, col_dev), jnp.float32)
    row_count = jnp.ones((row_dev,), jnp.float32)
    col_count = jnp.ones((col_dev,), jnp.float32)
    for sweep_number in range(SWEEPS):
        clipped = jnp.clip(
            (observations - row_effect[:, :, None] - col_effect[:, None, :]) / spread_scale,
            -HUBER_EDGE,
            HUBER_EDGE,
        )
        row_part = jnp.sum(weight[None] * clipped, axis=2)
        if sweep_number == 0:
            row_part, row_total = sum_rows((row_part, jnp.sum(weight, axis=1)))
            row_count = jnp.maximum(row_total, 1.0)
        else:
            row_part = sum_rows(row_part)
        row_effect = row_effect + huber_scale[:, None] * row_part / row_count[None, :]
        clipped = jnp.clip(
            (observations - row_effect[:, :, None] - col_effect[:, None, :]) / spread_scale,
            -HUBER_EDGE,
            HUBER_EDGE,
        )
        col_part = jnp.sum(weight[None] * clipped, axis=1)
        if sweep_number == 0:
            col_part, col_total = sum_columns((col_part, jnp.sum(weight, axis=0)))
            col_count = jnp.maximum(col_total, 1.0)
        else:
            col_part = sum_columns(col_part)
        col_effect = col_effect + huber_scale[:, None] * col_part / col_count[None, :]
    residual_field = weight[None] * (observations - row_effect[:, :, None] - col_effect[:, None, :])
    local_side = residual_field.reshape(fields, BLOCKS_DEV, BLOCK)
    row_place = (my_place * row_dev + jnp.arange(row_dev, dtype=jnp.int32)).astype(jnp.float32)
    col_place = (group_place * col_dev + jnp.arange(col_dev, dtype=jnp.int32)).astype(jnp.float32)
    location = jnp.stack([row_place[:, None] + jitter[0], col_place[None, :] + jitter[1]]).reshape(
        2, BLOCKS_DEV, BLOCK
    )
    group_map = owner_map[0]
    group_lists = neighbours[0]
    table = owned_table(group_map, sixteen_size, BLOCKS_DEV)
    my_ids = lax.dynamic_index_in_dim(table, my_place, 0, keepdims=False)
    my_targets = lax.dynamic_slice_in_dim(group_map, my_place * BLOCKS_DEV, BLOCKS_DEV)
    strip_ids = my_place * BLOCKS_DEV + block_numbers
    near_ids = lax.dynamic_slice_in_dim(group_lists, my_place * BLOCKS_DEV, BLOCKS_DEV)
    offsets = (near_ids - strip_ids[:, None] + total_strips // 2) % total_strips - total_strips // 2
    positions = (block_numbers[:, None] + REACH + offsets).reshape(-1)
    wider_places = padded(location, ((SIXTEEN, 1),), REACH)
    near_centres = jnp.take(wider_places, positions, axis=1).reshape(
        2, BLOCKS_DEV, NEIGHBOURS, BLOCK
    )

    def neighbour_values(direction):
        wider = padded(direction, ((SIXTEEN, 1),), REACH)
        return jnp.take(wider, positions, axis=1).reshape(fields, BLOCKS_DEV, NEIGHBOURS, BLOCK)

    def tiles_of(position):
        centre = lax.dynamic_index_in_dim(location, position, 1, keepdims=False)
        beside_all = lax.dynamic_index_in_dim(near_centres, position, 1, keepdims=False)
        return covariance(
            centre, jnp.concatenate([centre[:, None], beside_all], axis=1), strip_rows
        )

    stored_tiles = lax.map(tiles_of, block_numbers)

    def apply_operator(direction):
        near_values = neighbour_values(direction)

        def one_block(position):
            own = lax.dynamic_index_in_dim(direction, position, 1, keepdims=False)
            beside_all = lax.dynamic_index_in_dim(near_values, position, 1, keepdims=False)
            kernel = lax.dynamic_index_in_dim(stored_tiles, position, 0, keepdims=False)
            stacked = jnp.concatenate([(NEIGHBOURS + 1.0) * own[:, None], beside_all], axis=1)
            return NUGGET_TERM * own + jnp.einsum("fmb,mba->fa", stacked, kernel, precision=EXACT)

        return jnp.moveaxis(lax.map(one_block, block_numbers), 0, 1)

    solution_now = jnp.zeros_like(local_side)
    residual_now = local_side

    def two_products(observed_values, image):
        return (
            one_axis_at_a_time(
                jnp.sum(observed_values * observed_values, axis=(1, 2)), WIDE_SIXTEEN
            ),
            one_axis_at_a_time(jnp.sum(observed_values * image, axis=(1, 2)), WIDE_SIXTEEN),
        )

    image = apply_operator(residual_now)
    norm_now, product = two_products(residual_now, image)
    alpha = norm_now / product
    direction = residual_now
    along = image
    for number in range(ITERS):
        solution_now = solution_now + alpha[:, None, None] * direction
        residual_now = residual_now - alpha[:, None, None] * along
        if number + 1 < ITERS:
            image = apply_operator(residual_now)
            norm_next, product = two_products(residual_now, image)
            ratio = norm_next / norm_now
            alpha = norm_next / (product - ratio * norm_next / alpha)
            direction = residual_now + ratio[:, None, None] * direction
            along = image + ratio[:, None, None] * along
            norm_now = norm_next
    moved_solution, moved_residual = (
        exchange_in_pieces(outgoing(solution_now, my_targets, sixteen_size), SIXTEEN, 2, 1, 1),
        exchange_in_pieces(outgoing(residual_now, my_targets, sixteen_size), SIXTEEN, 2, 1, 1),
    )
    solution_now = incoming(moved_solution, my_ids, BLOCKS_DEV)
    residual_now = incoming(moved_residual, my_ids, BLOCKS_DEV)
    return (solution_now[None, None], residual_now[None, None])


def solution(mesh):
    finer = Mesh(mesh.devices.reshape(4, 2, 4, 4), ("wide_0", "wide_1", "sixteen_0", "sixteen_1"))
    in_specs = (
        P(None, SIXTEEN, WIDE),
        P(),
        P(SIXTEEN, WIDE),
        P(None, SIXTEEN, WIDE),
        P(WIDE, None),
        P(WIDE, None, None),
    )
    out_specs = (P(WIDE, SIXTEEN, None, None, None), P(WIDE, SIXTEEN, None, None, None))
    return jax.shard_map(
        on_device, mesh=finer, in_specs=in_specs, out_specs=out_specs, check_vma=False
    )
```

profile of v0, /device:TPU:0, one launch (start us, length us, event | category | flops | bytes accessed | tf_op | source)
XLA Modules:
  0.0 544.7 jit_solution(5934524895289707757)
XLA Ops:
  44.9 10.8 %all-to-all-done.2 = f32[16,64,128]{2,1,0:T(8,128)S(1)} async-done(((f32[16,64,128]{2,1,0:T(8,128)}), f32[16,64,128]{2,1,0:T(8,128)S(1)}, u32[]{:S(2)}, u32[]{:S(2)}) %all-to-all-start.2) | async-done | bytes 524320 | tf_op jit(solution)/shard_map/all_to_all | solution.py:29
  74.8 10.6 %all-to-all-done.5 = f32[16,64,128]{2,1,0:T(8,128)S(1)} async-done(((f32[16,64,128]{2,1,0:T(8,128)}), f32[16,64,128]{2,1,0:T(8,128)S(1)}, u32[]{:S(2)}, u32[]{:S(2)}) %all-to-all-start.5) | async-done | bytes 524320 | tf_op jit(solution)/shard_map/all_to_all | solution.py:29
  95.2 88.0 %while.32 = (s32[]{:T(128)}, f32[8,7,512,512]{3,2,1,0:T(8,128)}, s32[8]{0:T(128)S(1)}, f32[2,8,512]{2,0,1:T(2,128)S(1)}, f32[2,8,6,512]{3,0,2,1:T(2,128)S(1)}, /*index=5*/s32[]{:T(128)}, s32[]{:T(128)}, s32[]{:T(128)}) while((s32[]{:T(128)}, f32[8,7,512,512]{3,2,1,0:T(8,128)}, s32[8]{0:T(128)S(1)}, f32[2,8,512]{2,0,1:T(2,128)S(1)}, ...), condition=%wide.region_20.22_spmd, body=%wide.region_19.21_spmd.sunk | while | flops 34872324 | bytes 7553675 | solution.py:199
  98.0 8.2 %multiply_dynamic-update-slice_fusion.2 = f32[8,7,512,512]{3,2,1,0:T(8,128)} fusion(f32[8,7,512,512]{3,2,1,0:T(8,128)} %get-tuple-element.410, s32[]{:T(128)} %get-tuple-element.409, f32[512]{0:T(512)S(1)} %bitcast.210, f32[7,512]{1,0:T(8,128)S(1)} %get-tuple-element.386, f32[512]{0:T(512)S(1)} %bitcast.209, f32[7,512]{1,0:T(8,128)S(1)} %get-tuple-element.388), kind=kLoop, calls=%fused_computation.3.clone.1 | loop fusion | flops 34865152 | bytes 7373312 | tf_op jit(solution)/shard_map/while/body/jit(dynamic_update_index_in_dim)/dynamic_update_slice | solution.py:199
  109.0 8.2 %multiply_dynamic-update-slice_fusion.2 = f32[8,7,512,512]{3,2,1,0:T(8,128)} fusion(f32[8,7,512,512]{3,2,1,0:T(8,128)} %get-tuple-element.410, s32[]{:T(128)} %get-tuple-element.409, f32[512]{0:T(512)S(1)} %bitcast.210, f32[7,512]{1,0:T(8,128)S(1)} %get-tuple-element.386, f32[512]{0:T(512)S(1)} %bitcast.209, f32[7,512]{1,0:T(8,128)S(1)} %get-tuple-element.388), kind=kLoop, calls=%fused_computation.3.clone.1 | loop fusion | flops 34865152 | bytes 7373312 | tf_op jit(solution)/shard_map/while/body/jit(dynamic_update_index_in_dim)/dynamic_update_slice | solution.py:199
  119.9 8.2 %multiply_dynamic-update-slice_fusion.2 = f32[8,7,512,512]{3,2,1,0:T(8,128)} fusion(f32[8,7,512,512]{3,2,1,0:T(8,128)} %get-tuple-element.410, s32[]{:T(128)} %get-tuple-element.409, f32[512]{0:T(512)S(1)} %bitcast.210, f32[7,512]{1,0:T(8,128)S(1)} %get-tuple-element.386, f32[512]{0:T(512)S(1)} %bitcast.209, f32[7,512]{1,0:T(8,128)S(1)} %get-tuple-element.388), kind=kLoop, calls=%fused_computation.3.clone.1 | loop fusion | flops 34865152 | bytes 7373312 | tf_op jit(solution)/shard_map/while/body/jit(dynamic_update_index_in_dim)/dynamic_update_slice | solution.py:199
  130.9 8.2 %multiply_dynamic-update-slice_fusion.2 = f32[8,7,512,512]{3,2,1,0:T(8,128)} fusion(f32[8,7,512,512]{3,2,1,0:T(8,128)} %get-tuple-element.410, s32[]{:T(128)} %get-tuple-element.409, f32[512]{0:T(512)S(1)} %bitcast.210, f32[7,512]{1,0:T(8,128)S(1)} %get-tuple-element.386, f32[512]{0:T(512)S(1)} %bitcast.209, f32[7,512]{1,0:T(8,128)S(1)} %get-tuple-element.388), kind=kLoop, calls=%fused_computation.3.clone.1 | loop fusion | flops 34865152 | bytes 7373312 | tf_op jit(solution)/shard_map/while/body/jit(dynamic_update_index_in_dim)/dynamic_update_slice | solution.py:199
  141.9 8.3 %multiply_dynamic-update-slice_fusion.2 = f32[8,7,512,512]{3,2,1,0:T(8,128)} fusion(f32[8,7,512,512]{3,2,1,0:T(8,128)} %get-tuple-element.410, s32[]{:T(128)} %get-tuple-element.409, f32[512]{0:T(512)S(1)} %bitcast.210, f32[7,512]{1,0:T(8,128)S(1)} %get-tuple-element.386, f32[512]{0:T(512)S(1)} %bitcast.209, f32[7,512]{1,0:T(8,128)S(1)} %get-tuple-element.388), kind=kLoop, calls=%fused_computation.3.clone.1 | loop fusion | flops 34865152 | bytes 7373312 | tf_op jit(solution)/shard_map/while/body/jit(dynamic_update_index_in_dim)/dynamic_update_slice | solution.py:199
  153.0 8.2 %multiply_dynamic-update-slice_fusion.2 = f32[8,7,512,512]{3,2,1,0:T(8,128)} fusion(f32[8,7,512,512]{3,2,1,0:T(8,128)} %get-tuple-element.410, s32[]{:T(128)} %get-tuple-element.409, f32[512]{0:T(512)S(1)} %bitcast.210, f32[7,512]{1,0:T(8,128)S(1)} %get-tuple-element.386, f32[512]{0:T(512)S(1)} %bitcast.209, f32[7,512]{1,0:T(8,128)S(1)} %get-tuple-element.388), kind=kLoop, calls=%fused_computation.3.clone.1 | loop fusion | flops 34865152 | bytes 7373312 | tf_op jit(solution)/shard_map/while/body/jit(dynamic_update_index_in_dim)/dynamic_update_slice | solution.py:199
  164.0 8.3 %multiply_dynamic-update-slice_fusion.2 = f32[8,7,512,512]{3,2,1,0:T(8,128)} fusion(f32[8,7,512,512]{3,2,1,0:T(8,128)} %get-tuple-element.410, s32[]{:T(128)} %get-tuple-element.409, f32[512]{0:T(512)S(1)} %bitcast.210, f32[7,512]{1,0:T(8,128)S(1)} %get-tuple-element.386, f32[512]{0:T(512)S(1)} %bitcast.209, f32[7,512]{1,0:T(8,128)S(1)} %get-tuple-element.388), kind=kLoop, calls=%fused_computation.3.clone.1 | loop fusion | flops 34865152 | bytes 7373312 | tf_op jit(solution)/shard_map/while/body/jit(dynamic_update_index_in_dim)/dynamic_update_slice | solution.py:199
  175.0 8.2 %multiply_dynamic-update-slice_fusion.2 = f32[8,7,512,512]{3,2,1,0:T(8,128)} fusion(f32[8,7,512,512]{3,2,1,0:T(8,128)} %get-tuple-element.410, s32[]{:T(128)} %get-tuple-element.409, f32[512]{0:T(512)S(1)} %bitcast.210, f32[7,512]{1,0:T(8,128)S(1)} %get-tuple-element.386, f32[512]{0:T(512)S(1)} %bitcast.209, f32[7,512]{1,0:T(8,128)S(1)} %get-tuple-element.388), kind=kLoop, calls=%fused_computation.3.clone.1 | loop fusion | flops 34865152 | bytes 7373312 | tf_op jit(solution)/shard_map/while/body/jit(dynamic_update_index_in_dim)/dynamic_update_slice | solution.py:199
  196.4 91.7 %while.33 = (s32[]{:T(128)}, f32[8,64,512]{2,1,0:T(8,128)S(1)}, s32[8]{0:T(128)S(1)}, f32[64,8,512]{2,0,1:T(8,128)}, f32[64,8,6,512]{3,0,2,1:T(8,128)}, /*index=...) while((s32[]{:T(128)}, f32[8,64,512]{2,1,0:T(8,128)S(1)}, s32[8]{0:T(128)S(1)}, ...), condition=%wide.region_22.24_spmd, body=%wide.region_21.23_spmd.sunk | while | flops 1409581056 | bytes 10356371 | solution.py:211
  289.0 8.9 %all-reduce.5 = (f32[64]{0:T(128)S(1)}, f32[64]{0:T(128)S(1)}) all-reduce(f32[64]{0:T(128)S(1)} %get-tuple-element.264, f32[64]{0:T(128)S(1)} %fusion.54), channel_id=1, replica_groups=mesh['wide_0'=4,'wide_1'=2,'sixteen_0'=4,'sixteen_1'=4] {'wide_0'}, use_global_device_ids=true, to_apply=%region_15.16 | all-reduce | flops 128 | bytes 1024 | tf_op jit(solution)/shard_map/psum | solution.py:53
  300.3 7.7 %all-reduce.3 = (f32[64]{0:T(128)S(1)}, f32[64]{0:T(128)S(1)}) all-reduce(f32[64]{0:T(128)S(1)} %get-tuple-element.260, f32[64]{0:T(128)S(1)} %get-tuple-element.261), channel_id=1, replica_groups=mesh['wide_0'=4,'wide_1'=2,'sixteen_0'=4,'sixteen_1'=4] {'sixteen_0'}, use_global_device_ids=true, to_apply=%region_17.18 | all-reduce | flops 128 | bytes 1024 | tf_op jit(solution)/shard_map/psum | solution.py:53
  308.0 8.3 %all-reduce.1 = (f32[64]{0:T(128)S(1)}, f32[64]{0:T(128)S(1)}) all-reduce(f32[64]{0:T(128)S(1)} %get-tuple-element.252, f32[64]{0:T(128)S(1)} %get-tuple-element.253), channel_id=1, replica_groups=mesh['wide_0'=4,'wide_1'=2,'sixteen_0'=4,'sixteen_1'=4] {'sixteen_1'}, use_global_device_ids=true, to_apply=%region_18.19 | all-reduce | flops 128 | bytes 1024 | tf_op jit(solution)/shard_map/psum | solution.py:53
  322.6 8.1 %collective-permute-done.4 = f32[64,4,512]{2,0,1:T(8,128)} collective-permute-done((f32[64,4,512]{2,0,1:T(8,128)S(1)}, f32[64,4,512]{2,0,1:T(8,128)}, u32[]{:S(2)}, u32[]{:S(2)}) %collective-permute-start.4) | collective-permute-done | bytes 524320 | tf_op jit(solution)/shard_map/ppermute | solution.py:46
  343.9 86.8 %while.34 = (s32[]{:T(128)}, f32[8,64,512]{2,1,0:T(8,128)}, s32[8]{0:T(128)S(1)}, f32[64,8,512]{2,0,1:T(8,128)S(1)}, f32[64,8,6,512]{3,0,2,1:T(8,128)}, /*index=...) while((s32[]{:T(128)}, f32[8,64,512]{2,1,0:T(8,128)}, s32[8]{0:T(128)S(1)}, ...), condition=%wide.region_34.36_spmd, body=%wide.region_33.35_spmd.sunk | while | flops 1409581056 | bytes 10356371 | solution.py:211
  432.1 8.6 %all-reduce.4 = (f32[64]{0:T(128)S(1)}, f32[64]{0:T(128)S(1)}) all-reduce(f32[64]{0:T(128)S(1)} %get-tuple-element.209, f32[64]{0:T(128)S(1)} %get-tuple-element.208), channel_id=1, replica_groups=mesh['wide_0'=4,'wide_1'=2,'sixteen_0'=4,'sixteen_1'=4] {'wide_0'}, use_global_device_ids=true, to_apply=%region_29.31 | all-reduce | flops 128 | bytes 1024 | tf_op jit(solution)/shard_map/psum | solution.py:53
  443.2 8.1 %all-reduce.2 = (f32[64]{0:T(128)S(1)}, f32[64]{0:T(128)S(1)}) all-reduce(f32[64]{0:T(128)S(1)} %get-tuple-element.258, f32[64]{0:T(128)S(1)} %get-tuple-element.259), channel_id=1, replica_groups=mesh['wide_0'=4,'wide_1'=2,'sixteen_0'=4,'sixteen_1'=4] {'sixteen_0'}, use_global_device_ids=true, to_apply=%region_31.33 | all-reduce | flops 128 | bytes 1024 | tf_op jit(solution)/shard_map/psum | solution.py:53
  451.3 12.9 %all-reduce = (f32[64]{0:T(128)S(1)}, f32[64]{0:T(128)S(1)}) all-reduce(f32[64]{0:T(128)S(1)} %get-tuple-element.250, f32[64]{0:T(128)S(1)} %get-tuple-element.251), channel_id=1, replica_groups=mesh['wide_0'=4,'wide_1'=2,'sixteen_0'=4,'sixteen_1'=4] {'sixteen_1'}, use_global_device_ids=true, to_apply=%region_32.34 | all-reduce | flops 128 | bytes 1024 | tf_op jit(solution)/shard_map/psum | solution.py:53
  476.0 12.8 %all-to-all-done.8 = f32[16,32,1,512]{3,1,2,0:T(8,128)S(1)} async-done(((f32[16,32,1,512]{3,1,2,0:T(8,128)}), f32[16,32,1,512]{3,1,2,0:T(8,128)S(1)}, u32[]{:S(2)}, u32[]{:S(2)}) %all-to-all-start.8) | async-done | bytes 1048608 | tf_op jit(solution)/shard_map/all_to_all | solution.py:79
  496.8 9.4 %all-to-all-done.9 = f32[16,32,1,512]{3,1,2,0:T(8,128)S(1)} async-done(((f32[16,32,1,512]{3,1,2,0:T(8,128)}), f32[16,32,1,512]{3,1,2,0:T(8,128)S(1)}, u32[]{:S(2)}, u32[]{:S(2)}) %all-to-all-start.9) | async-done | bytes 1048608 | tf_op jit(solution)/shard_map/all_to_all | solution.py:79
  512.7 10.5 %all-to-all-done.6 = f32[16,32,1,512]{3,1,2,0:T(8,128)S(1)} async-done(((f32[16,32,1,512]{3,1,2,0:T(8,128)}), f32[16,32,1,512]{3,1,2,0:T(8,128)S(1)}, u32[]{:S(2)}, u32[]{:S(2)}) %all-to-all-start.6) | async-done | bytes 1048608 | tf_op jit(solution)/shard_map/all_to_all | solution.py:79
  532.1 9.0 %all-to-all-done.7 = f32[16,32,1,512]{3,1,2,0:T(8,128)} async-done(((f32[16,32,1,512]{3,1,2,0:T(8,128)}), f32[16,32,1,512]{3,1,2,0:T(8,128)}, u32[]{:S(2)}, u32[]{:S(2)}) %all-to-all-start.7) | async-done | bytes 1048608 | tf_op jit(solution)/shard_map/all_to_all | solution.py:79
  (271 shorter events, 306.3 us)
Async XLA Ops:
  0.6 55.8 %copy-start.2 = (f32[64,32,128]{2,1,0:T(8,128)S(1)}, f32[64,32,128]{2,1,0:T(8,128)}, u32[]{:S(2)}) copy-start(f32[64,32,128]{2,1,0:T(8,128)} %param.14) | copy-start | bytes 3145732
  0.7 67.9 %copy-start.9 = (f32[64]{0:T(128)S(1)}, f32[64]{0:T(128)}, u32[]{:S(2)}) copy-start(f32[64]{0:T(128)} %param.15) | copy-start | bytes 772
  1.6 72.1 %collective-permute-start.2 = (f32[2,4,512]{2,0,1:T(2,128)S(1)}, f32[2,4,512]{2,0,1:T(2,128)S(1)}, u32[]{:S(2)}, u32[]{:S(2)}) collective-permute-start(f32[2,4,512]{2,0,1:T(2,128)S(1)} %get-tuple-element.282), channel_id=1, source_target_pairs={{0,1},{1,2},{2,3},{3,4},{4,5},{5,6},{6,7},{7,8},{8,9},{9,10},{10,1... | collective-permute-start | bytes 49160 | tf_op jit(solution)/shard_map/ppermute | solution.py:46
  3.3 70.5 %collective-permute-start.3 = (f32[2,4,512]{2,0,1:T(2,128)S(1)}, f32[2,4,512]{2,0,1:T(2,128)S(1)}, u32[]{:S(2)}, u32[]{:S(2)}) collective-permute-start(f32[2,4,512]{2,0,1:T(2,128)S(1)} %get-tuple-element.283), channel_id=1, source_target_pairs={{1,0},{2,1},{3,2},{4,3},{5,4},{6,5},{7,6},{8,7},{9,8},{10,9},{11,1... | collective-permute-start | bytes 49160 | tf_op jit(solution)/shard_map/ppermute | solution.py:47
  9.5 9.7 %all-to-all-start.1 = ((f32[8,1,32]{2,1,0:T(1,128)}), f32[8,1,32]{2,1,0:T(1,128)S(1)}, u32[]{:S(2)}, u32[]{:S(2)}) async-start(f32[8,1,32]{2,1,0:T(1,128)} %broadcast_in_dim.42), calls=%async_computation.1 | async-start | bytes 8192 | tf_op jit(solution)/shard_map/all_to_all | solution.py:29
  19.2 9.3 %all-to-all-start = ((f32[8,1,2048]{2,1,0:T(1,128)}), f32[8,1,2048]{2,1,0:T(1,128)S(1)}, u32[]{:S(2)}, u32[]{:S(2)}) async-start(f32[8,1,2048]{2,1,0:T(1,128)} %reshape.563), calls=%async_computation | async-start | bytes 131072 | tf_op jit(solution)/shard_map/all_to_all | solution.py:29
  29.1 11.1 %all-to-all-start.3 = ((f32[16,1,128]{2,1,0:T(1,128)}), f32[16,1,128]{2,1,0:T(1,128)S(1)}, u32[]{:S(2)}, u32[]{:S(2)}) async-start(f32[16,1,128]{2,1,0:T(1,128)} %broadcast_in_dim.44), calls=%async_computation.3 | async-start | bytes 16384 | tf_op jit(solution)/shard_map/all_to_all | solution.py:29
  41.0 14.7 %all-to-all-start.2 = ((f32[16,64,128]{2,1,0:T(8,128)}), f32[16,64,128]{2,1,0:T(8,128)S(1)}, u32[]{:S(2)}, u32[]{:S(2)}) async-start(f32[16,64,128]{2,1,0:T(8,128)} %broadcast_in_dim.43), calls=%async_computation.2 | async-start | bytes 1048576 | tf_op jit(solution)/shard_map/all_to_all | solution.py:29
  58.8 8.9 %all-to-all-start.4 = ((f32[8,1,2048]{2,1,0:T(1,128)}), f32[8,1,2048]{2,1,0:T(1,128)S(1)}, u32[]{:S(2)}, u32[]{:S(2)}) async-start(f32[8,1,2048]{2,1,0:T(1,128)} %reshape.565), calls=%async_computation.4 | async-start | bytes 131072 | tf_op jit(solution)/shard_map/all_to_all | solution.py:29
  70.2 15.3 %all-to-all-start.5 = ((f32[16,64,128]{2,1,0:T(8,128)}), f32[16,64,128]{2,1,0:T(8,128)S(1)}, u32[]{:S(2)}, u32[]{:S(2)}) async-start(f32[16,64,128]{2,1,0:T(8,128)} %broadcast_in_dim.46), calls=%async_computation.5 | async-start | bytes 1048576 | tf_op jit(solution)/shard_map/all_to_all | solution.py:29
  86.9 229.4 %copy-start.3 = (f32[64,8,512]{2,1,0:T(8,128)}, f32[64,8,512]{2,1,0:T(8,128)S(1)}, u32[]{:S(2)}) copy-start(f32[64,8,512]{2,1,0:T(8,128)S(1)} %reshape.522) | copy-start | bytes 3145732
  89.8 93.4 %collective-permute-start = (f32[64,4,512]{2,0,1:T(8,128)S(1)}, f32[64,4,512]{2,0,1:T(8,128)S(1)}, u32[]{:S(2)}, u32[]{:S(2)}) collective-permute-start(f32[64,4,512]{2,0,1:T(8,128)S(1)} %get-tuple-element.280), channel_id=1, source_target_pairs={{0,1},{1,2},{2,3},{3,4},{4,5},{5,6},{6,7},{7,8},{8,9},{9,10},{10,1... | collective-permute-start | bytes 1572872 | tf_op jit(solution)/shard_map/ppermute | solution.py:46
  90.4 93.5 %collective-permute-start.1 = (f32[64,4,512]{2,0,1:T(8,128)S(1)}, f32[64,4,512]{2,0,1:T(8,128)}, u32[]{:S(2)}, u32[]{:S(2)}) collective-permute-start(f32[64,4,512]{2,0,1:T(8,128)S(1)} %get-tuple-element.281), channel_id=1, source_target_pairs={{1,0},{2,1},{3,2},{4,3},{5,4},{6,5},{7,6},{8,7},{9,8},{10,9},{11,1... | collective-permute-start | bytes 1572872 | tf_op jit(solution)/shard_map/ppermute | solution.py:47
  288.2 42.5 %copy-start.5 = (f32[8,64,512]{2,1,0:T(8,128)}, f32[8,64,512]{2,1,0:T(8,128)S(1)}, u32[]{:S(2)}) copy-start(f32[8,64,512]{2,1,0:T(8,128)S(1)} %get-tuple-element.134) | copy-start | bytes 3145732
  288.2 34.3 %copy-start.10 = (s32[1,128]{1,0:T(1,128)S(1)}, s32[1,128]{1,0:T(1,128)}, u32[]{:S(2)}) copy-start(s32[1,128]{1,0:T(1,128)} %param.18) | copy-start | bytes 1540
  317.1 13.6 %collective-permute-start.4 = (f32[64,4,512]{2,0,1:T(8,128)S(1)}, f32[64,4,512]{2,0,1:T(8,128)}, u32[]{:S(2)}, u32[]{:S(2)}) collective-permute-start(f32[64,4,512]{2,0,1:T(8,128)S(1)} %get-tuple-element.278), channel_id=1, source_target_pairs={{0,1},{1,2},{2,3},{3,4},{4,5},{5,6},{6,7},{7,8},{8,9},{9,10},{10,1... | collective-permute-start | bytes 1572872 | tf_op jit(solution)/shard_map/ppermute | solution.py:46
  318.6 12.0 %collective-permute-start.5 = (f32[64,4,512]{2,0,1:T(8,128)S(1)}, f32[64,4,512]{2,0,1:T(8,128)}, u32[]{:S(2)}, u32[]{:S(2)}) collective-permute-start(f32[64,4,512]{2,0,1:T(8,128)S(1)} %get-tuple-element.279), channel_id=1, source_target_pairs={{1,0},{2,1},{3,2},{4,3},{5,4},{6,5},{7,6},{8,7},{9,8},{10,9},{11,1... | collective-permute-start | bytes 1572872 | tf_op jit(solution)/shard_map/ppermute | solution.py:47
  343.9 120.3 %copy-start.4 = (f32[64,8,512]{2,1,0:T(8,128)S(1)}, f32[64,8,512]{2,1,0:T(8,128)}, u32[]{:S(2)}) copy-start(f32[64,8,512]{2,1,0:T(8,128)} %copy-done.3) | copy-start | bytes 3145732
  343.9 120.3 %copy-start.6 = (f32[8,64,512]{2,1,0:T(8,128)S(1)}, f32[8,64,512]{2,1,0:T(8,128)}, u32[]{:S(2)}) copy-start(f32[8,64,512]{2,1,0:T(8,128)} %copy-done.5) | copy-start | bytes 3145732
  468.9 23.5 %copy-start.7 = (f32[64,8,512]{2,0,1:T(8,128)S(1)}, f32[64,8,512]{2,0,1:T(8,128)}, u32[]{:S(2)}) copy-start(f32[64,8,512]{2,0,1:T(8,128)} %get-tuple-element.277) | copy-start | bytes 3145732
  470.8 18.0 %all-to-all-start.8 = ((f32[16,32,1,512]{3,1,2,0:T(8,128)}), f32[16,32,1,512]{3,1,2,0:T(8,128)S(1)}, u32[]{:S(2)}, u32[]{:S(2)}) async-start(f32[16,32,1,512]{3,1,2,0:T(8,128)} %copy.127), calls=%async_computation.8 | async-start | bytes 2097152 | tf_op jit(solution)/shard_map/all_to_all | solution.py:79
  488.8 17.4 %all-to-all-start.9 = ((f32[16,32,1,512]{3,1,2,0:T(8,128)}), f32[16,32,1,512]{3,1,2,0:T(8,128)S(1)}, u32[]{:S(2)}, u32[]{:S(2)}) async-start(f32[16,32,1,512]{3,1,2,0:T(8,128)} %copy.128), calls=%async_computation.9 | async-start | bytes 2097152 | tf_op jit(solution)/shard_map/all_to_all | solution.py:79
  506.2 17.0 %all-to-all-start.6 = ((f32[16,32,1,512]{3,1,2,0:T(8,128)}), f32[16,32,1,512]{3,1,2,0:T(8,128)S(1)}, u32[]{:S(2)}, u32[]{:S(2)}) async-start(f32[16,32,1,512]{3,1,2,0:T(8,128)} %copy.122), calls=%async_computation.6 | async-start | bytes 2097152 | tf_op jit(solution)/shard_map/all_to_all | solution.py:79
  523.2 18.0 %all-to-all-start.7 = ((f32[16,32,1,512]{3,1,2,0:T(8,128)}), f32[16,32,1,512]{3,1,2,0:T(8,128)}, u32[]{:S(2)}, u32[]{:S(2)}) async-start(f32[16,32,1,512]{3,1,2,0:T(8,128)} %copy.123), calls=%async_computation.7 | async-start | bytes 2097152 | tf_op jit(solution)/shard_map/all_to_all | solution.py:79
  (3 other events, 31.2 us)
where the time goes:
time: 548 us; the launch traced here: 545 us
  matrix products  120 us (22%)
  other arithmetic  110 us (20%)
  waiting for transfers between devices  87 us (16%)
  local copies, waits for them, and re-layouts  66 us (12%)
  blocking collectives  59.4 us (11%)
  starting transfers between devices  55.2 us (10%)
  loops' own time  45.7 us (8%)
    dot_general x16, matrix products, one_block(): jnp.einsum('fmb,mba->fa', stacked, kernel, precision=EXACT)  114 us
    dynamic_update_slice x8, other arithmetic, on_device(): stored_tiles = lax.map(tiles_of, block_numbers)  65.8 us
    psum x8, blocking collectives, one_axis_at_a_time(): return functools.reduce(lax.psum, axes, shard)  59.4 us
    all_to_all x4, waiting for transfers between devices, exchange_in_pieces(): lax.all_to_all(section, axis, split_axis=0, concat_axis=0, tiled=True)  41.7 us
    all_to_all x6, waiting for transfers between devices, sent_to_all(): lax.all_to_all(jnp.broadcast_to(shard[None], (peers, *shard.shape)), axis...  37.2 us
    another operation x2, loops' own time, apply_operator(): return jnp.moveaxis(lax.map(one_block, block_numbers), 0, 1)  29.2 us
    all_to_all x6, starting transfers between devices, sent_to_all(): lax.all_to_all(jnp.broadcast_to(shard[None], (peers, *shard.shape)), axis...  22.4 us
    squeeze x16, local copies, waits for them, and re-layouts, one_block(): lax.dynamic_index_in_dim(near_values, position, 1, keepdims=False)  19.1 us
  transfers between devices with their start and end apart: 16, of which 11 were waited for; matrix products, arithmetic and copies ran while one was open for 19% of the time, Pallas kernels for 0%

commit v1 on v0

v1 whole, which is shorter than its diff:
```python
import functools

import jax
import jax.numpy as jnp
from jax import lax
from jax.experimental import pallas as pl
from jax.experimental.pallas import tpu as pltpu
from jax.sharding import Mesh
from jax.sharding import PartitionSpec as P

BLOCK = 512
BLOCKS_DEV = 8
REACH = 4
NEIGHBOURS = 6
PAIRED = NEIGHBOURS // 2
SWEEPS = 2
STRIP = 4
COL_DEV = 128
WIDE = ("wide_0", "wide_1")
SIXTEEN = ("sixteen_0", "sixteen_1")

HUBER_EDGE = 1.345
SILL_TERM = 0.02
ROOT_THREE = 1.7320508075688772
SPREAD = 2.0 * STRIP
CUTOFF = 6.0 * STRIP
BAND = 24
GROUP = 16

OWN_TILES = BLOCKS_DEV + PAIRED * BLOCKS_DEV - 6
HALO_TILES = 2 * (2 + 3 + 4)


def sent_to_all(shard, axis):
    peers = lax.axis_size(axis)
    return lax.all_to_all(
        jnp.broadcast_to(shard[None], (peers, *shard.shape)), axis, 0, 0, tiled=True
    )


def over_copies(shard, axis):
    return jnp.sum(sent_to_all(shard, axis), axis=0)


def beside(shard, width):
    peers, length = lax.axis_size(SIXTEEN), shard.shape[0]
    up = [(i, (i + 1) % peers) for i in range(peers)]
    down = [(j, i) for i, j in up]
    before = lax.ppermute(lax.slice_in_dim(shard, length - width, length, axis=0), SIXTEEN, up)
    after = lax.ppermute(lax.slice_in_dim(shard, 0, width, axis=0), SIXTEEN, down)
    return before, after


def owned_table(group_map, owners, per_owner):
    total_strips = group_map.shape[0]
    member = (group_map[None, :] == jnp.arange(owners, dtype=jnp.int32)[:, None]).astype(jnp.int32)
    ranked = jnp.cumsum(member, axis=1, dtype=jnp.int32) - 1
    slot_hit = (ranked[:, :, None] == jnp.arange(per_owner, dtype=jnp.int32)[None, None, :]).astype(
        jnp.int32
    ) * member[:, :, None]
    numbers = jnp.arange(total_strips, dtype=jnp.int32)
    return jnp.sum(slot_hit * numbers[None, :, None], axis=1, dtype=jnp.int32)


def tile_lists(first_list, first_block, total):
    steps = jnp.arange(1, REACH + 1, dtype=jnp.int32)
    held = jnp.any(
        first_list[None, :] == ((first_block + steps) % total)[:, None], axis=1
    )
    missing = jnp.min(jnp.where(held, REACH + 1, steps))
    offsets = [k + (missing <= k).astype(jnp.int32) for k in range(1, PAIRED + 1)]
    d1, d2, d3 = offsets
    t = jnp.arange(OWN_TILES - BLOCKS_DEV, dtype=jnp.int32)
    n1, n2, n3 = BLOCKS_DEV - d1, BLOCKS_DEV - d2, BLOCKS_DEV - d3
    count = n1 + n2 + n3
    t = jnp.minimum(t, count - 1)
    a = jnp.where(t < n1, t, jnp.where(t < n1 + n2, t - n1, t - n1 - n2))
    b = a + jnp.where(t < n1, d1, jnp.where(t < n1 + n2, d2, d3))
    own = jnp.arange(BLOCKS_DEV, dtype=jnp.int32)
    own_a, own_b = jnp.concatenate([own, a]), jnp.concatenate([own, b])
    own_count = BLOCKS_DEV + count
    half = HALO_TILES // 2
    t = jnp.arange(half, dtype=jnp.int32)
    halo = d1 + d2 + d3
    t = jnp.minimum(t, halo - 1)
    step = jnp.where(t < d1, d1, jnp.where(t < d1 + d2, d2, d3))
    pos = jnp.where(t < d1, t, jnp.where(t < d1 + d2, t - d1, t - d1 - d2))
    left_a, left_b = pos, pos - step
    right_a, right_b = BLOCKS_DEV - 1 - pos, BLOCKS_DEV - 1 - pos + step
    halo_a = jnp.concatenate([left_a, right_a])
    halo_b = jnp.concatenate([left_b, right_b])
    live = jnp.concatenate(
        [
            jnp.arange(OWN_TILES, dtype=jnp.int32) < own_count,
            jnp.tile(jnp.arange(half, dtype=jnp.int32) < halo, 2),
        ]
    ).astype(jnp.int32)
    return jnp.concatenate([own_a, halo_a]), jnp.concatenate([own_b, halo_b]), live


def tiles_kernel(a_ref, b_ref, live_ref, rows_ref, cols_ref, hi_ref, lo_ref):
    t = pl.program_id(0)

    @pl.when(live_ref[t] == 1)
    def _():
        one, other = a_ref[t] + REACH, b_ref[t] + REACH
        sill = jnp.where(one == other, (NEIGHBOURS + 1.0) * SILL_TERM, SILL_TERM)
        lane = lax.broadcasted_iota(jnp.int32, (GROUP, COL_DEV), 1)
        to = rows_ref[one]
        frm = cols_ref[other]
        a, b = ROOT_THREE * CUTOFF / SPREAD, 4.0
        for rb in range(STRIP):
            row_b = jnp.broadcast_to(frm[:, rb : rb + 1], (COL_DEV, COL_DEV))
            col_b = jnp.broadcast_to(frm[:, STRIP + rb : STRIP + rb + 1], (COL_DEV, COL_DEV))
            for u in range(COL_DEV // 2 // GROUP):
                lo_s = slice(GROUP * u, GROUP * (u + 1))
                hi_s = slice(64 + GROUP * u, 64 + GROUP * (u + 1))
                near = (lane >= GROUP * u - BAND) & (lane < GROUP * (u + 1) + BAND)
                one_m = jnp.where(near, 1.0, 0.0).astype(jnp.bfloat16)
                other_m = jnp.where(near, 0.0, 1.0).astype(jnp.bfloat16)
                row_s = jnp.where(near, row_b[lo_s], row_b[hi_s])
                col_s = jnp.where(near, col_b[lo_s], col_b[hi_s])
                for ra in range(STRIP):
                    dr = row_s - to[ra : ra + 1]
                    dc = col_s - to[STRIP + ra : STRIP + ra + 1]
                    square = dr * dr + dc * dc
                    far = square * lax.rsqrt(jnp.maximum(square, 1e-30))
                    fading = jnp.maximum(1.0 - far, 0.0)
                    fading = fading * fading
                    fading = fading * fading
                    shape = (1.0 + a * far) * (sill + (sill * b) * far)
                    value = shape * fading * jnp.exp(-a * far)
                    hi = value.astype(jnp.bfloat16)
                    lo = (value - hi.astype(jnp.float32)).astype(jnp.bfloat16)
                    lanes = slice(COL_DEV * ra, COL_DEV * (ra + 1))
                    top = rb * COL_DEV + GROUP * u
                    hi_ref[0, top : top + GROUP, lanes] = hi * one_m
                    hi_ref[0, top + 64 : top + 64 + GROUP, lanes] = hi * other_m
                    lo_ref[0, top : top + GROUP, lanes] = lo * one_m
                    lo_ref[0, top + 64 : top + 64 + GROUP, lanes] = lo * other_m


def covariance_tiles(one, other, live, rows, cols):
    count = one.shape[0]
    tile = pl.BlockSpec((1, BLOCK, BLOCK), lambda t, *_: (t, 0, 0))
    whole = lambda shape: pl.BlockSpec(shape, lambda t, *_: (0, 0, 0))
    shape = jax.ShapeDtypeStruct((count, BLOCK, BLOCK), jnp.bfloat16)
    return pl.pallas_call(
        tiles_kernel,
        grid_spec=pltpu.PrefetchScalarGridSpec(
            num_scalar_prefetch=3,
            grid=(count,),
            in_specs=[whole(rows.shape), whole(cols.shape)],
            out_specs=[tile, tile],
        ),
        out_shape=[shape, shape],
        compiler_params=pltpu.CompilerParams(vmem_limit_bytes=32 << 20),
        name="tiles",
    )(one, other, live, rows, cols)


def halves(v):
    hi = v.astype(jnp.bfloat16)
    lo = (v - hi.astype(jnp.float32)).astype(jnp.bfloat16)
    return hi, lo


NN = (((1,), (0,)), ((), ()))
NT = (((1,), (1,)), ((), ()))


def product(both, hi_tile, lo_tile, dims):
    fields = both.shape[0] // 2
    main = lax.dot_general(both, hi_tile, dims, preferred_element_type=jnp.float32)
    rest = lax.dot_general(both[:fields], lo_tile, dims, preferred_element_type=jnp.float32)
    return main[:fields] + (main[fields:] + rest)


def own_kernel(a_ref, b_ref, live_ref, v_ref, hi_ref, lo_ref, out_ref, both_ref):
    t = pl.program_id(0)
    fields = v_ref.shape[1]

    @pl.when(t == 0)
    def _():
        for g in range(BLOCKS_DEV):
            hi, lo = halves(v_ref[g])
            both_ref[g, :fields] = hi
            both_ref[g, fields:] = lo

    @pl.when(t < BLOCKS_DEV)
    def _():
        out_ref[t] = product(both_ref[t], hi_ref[0], lo_ref[0], NN)

    @pl.when((t >= BLOCKS_DEV) & (live_ref[t] == 1))
    def _():
        one, other = a_ref[t], b_ref[t]
        out_ref[one] += product(both_ref[other], hi_ref[0], lo_ref[0], NN)
        out_ref[other] += product(both_ref[one], hi_ref[0], lo_ref[0], NT)


def halo_kernel(
    a_ref, b_ref, live_ref, before_ref, after_ref, part_ref, hi_ref, lo_ref, out_ref, both_ref
):
    t = pl.program_id(0)
    fields = before_ref.shape[1]

    @pl.when(t == 0)
    def _():
        for g in range(REACH):
            for side, ref in enumerate((before_ref, after_ref)):
                hi, lo = halves(ref[g])
                both_ref[side * REACH + g, :fields] = hi
                both_ref[side * REACH + g, fields:] = lo
        out_ref[...] = part_ref[...]

    @pl.when(live_ref[t + OWN_TILES] == 1)
    def _():
        one, other = a_ref[t + OWN_TILES], b_ref[t + OWN_TILES]
        slot = jnp.where(other < 0, other + REACH, other - BLOCKS_DEV + REACH)
        out_ref[one] += product(both_ref[slot], hi_ref[0], lo_ref[0], NN)


def own_product(one, other, live, v, hi, lo):
    blocks, fields, _ = v.shape
    whole = pl.BlockSpec(v.shape, lambda t, *_: (0, 0, 0))
    tile = pl.BlockSpec((1, BLOCK, BLOCK), lambda t, *_: (t, 0, 0))
    return pl.pallas_call(
        own_kernel,
        grid_spec=pltpu.PrefetchScalarGridSpec(
            num_scalar_prefetch=3,
            grid=(OWN_TILES,),
            in_specs=[whole, tile, tile],
            out_specs=whole,
            scratch_shapes=[pltpu.VMEM((blocks, 2 * fields, BLOCK), jnp.bfloat16)],
        ),
        out_shape=jax.ShapeDtypeStruct(v.shape, jnp.float32),
        compiler_params=pltpu.CompilerParams(vmem_limit_bytes=32 << 20),
        name="own",
    )(one, other, live, v, hi, lo)


def halo_product(one, other, live, before, after, part, hi, lo):
    blocks, fields, _ = part.shape
    whole = lambda x: pl.BlockSpec(x.shape, lambda t, *_: (0, 0, 0))
    tile = pl.BlockSpec((1, BLOCK, BLOCK), lambda t, *_: (t + OWN_TILES, 0, 0))
    return pl.pallas_call(
        halo_kernel,
        grid_spec=pltpu.PrefetchScalarGridSpec(
            num_scalar_prefetch=3,
            grid=(HALO_TILES,),
            in_specs=[whole(before), whole(after), whole(part), tile, tile],
            out_specs=whole(part),
            scratch_shapes=[pltpu.VMEM((2 * REACH, 2 * fields, BLOCK), jnp.bfloat16)],
        ),
        out_shape=jax.ShapeDtypeStruct(part.shape, jnp.float32),
        compiler_params=pltpu.CompilerParams(vmem_limit_bytes=32 << 20),
        name="halo",
    )(one, other, live, before, after, part, hi, lo)


def sum_rows(parts):
    return jax.tree.map(lambda part: over_copies(part, WIDE), parts)


def sum_columns(parts):
    return jax.tree.map(lambda part: over_copies(part, SIXTEEN), parts)


def combine_kernel(src_ref, scale_ref, *refs):
    ins, (x_ref, r_ref) = refs[:-2], refs[-2:]
    scale = scale_ref[...]
    for j in range(BLOCKS_DEV):
        r0, m1, m2 = (ref[0] for ref in ins[3 * j : 3 * j + 3])
        x_ref[:, j, :] = scale[:, 0:1] * r0 + scale[:, 1:2] * m1
        r_ref[:, j, :] = scale[:, 2:3] * r0 + scale[:, 3:4] * m1 + scale[:, 4:5] * m2


def combined(sources, scale, r0, m1, m2):
    fields = r0.shape[1]
    part = 8
    ins, specs = [], []
    for j in range(BLOCKS_DEV):
        for v in (r0, m1, m2):
            ins.append(v)
            specs.append(
                pl.BlockSpec(
                    (1, part, BLOCK), functools.partial(lambda j, i, s: (s[j], i, 0), j)
                )
            )
    out = pl.BlockSpec((part, BLOCKS_DEV, BLOCK), lambda i, s: (i, 0, 0))
    shape = jax.ShapeDtypeStruct((fields, BLOCKS_DEV, BLOCK), jnp.float32)
    return pl.pallas_call(
        combine_kernel,
        grid_spec=pltpu.PrefetchScalarGridSpec(
            num_scalar_prefetch=1,
            grid=(fields // part,),
            in_specs=[pl.BlockSpec((part, 8), lambda i, s: (i, 0))] + specs,
            out_specs=[out, out],
        ),
        out_shape=[shape, shape],
        compiler_params=pltpu.CompilerParams(vmem_limit_bytes=32 << 20),
        name="combine",
    )(sources, scale, *ins)


def spread_kernel(slot_ref, v_ref, out_ref):
    out_ref[...] = v_ref[...]


def to_owners(v, targets):
    owners = lax.axis_size(SIXTEEN)
    _, fields, _ = v.shape
    block = (1, fields, BLOCK)
    slots = pl.pallas_call(
        spread_kernel,
        grid_spec=pltpu.PrefetchScalarGridSpec(
            num_scalar_prefetch=1,
            grid=(BLOCKS_DEV,),
            in_specs=[pl.BlockSpec(block, lambda g, s: (g, 0, 0))],
            out_specs=pl.BlockSpec(block, lambda g, s: (s[g], 0, 0)),
        ),
        out_shape=jax.ShapeDtypeStruct((owners, fields, BLOCK), jnp.float32),
        name="spread",
    )(targets, v)
    return lax.all_to_all(slots, SIXTEEN, 0, 0, tiled=True)


def step_scales(h00, h01, h11, h12):
    mu = h01 / h00
    var = (h11 - mu * h01) / h00
    a0 = 1.0 / (1.0 + mu)
    beta = var * a0 * a0
    skew = (h12 - mu * h11 - mu * (h11 - mu * h01)) / h00
    a1 = var / (var + skew - var * var * a0)
    x_r0 = a0 + a1 * beta + a1 * a0 * mu
    x_m1 = -a1 * a0
    r_r0 = a0 * mu * (1.0 - a1) - a1 * beta
    r_m1 = -a0 * (1.0 - a1) - a1 * a0 * mu - a1 * beta
    r_m2 = a1 * a0
    zero = jnp.zeros_like(mu)
    return jnp.stack([x_r0, x_m1, r_r0, r_m1, r_m2, zero, zero, zero], axis=1)


def on_device(observations, huber_scale, observed, jitter, owner_map, neighbours):
    fields, row_dev, col_dev = observations.shape
    sixteen_size = lax.axis_size(SIXTEEN)
    my_place = lax.axis_index(SIXTEEN)
    group_place = lax.axis_index(WIDE)
    total_strips = BLOCKS_DEV * sixteen_size
    group_map = owner_map[0]
    group_lists = neighbours[0]
    table = owned_table(group_map, sixteen_size, BLOCKS_DEV)
    my_ids = lax.dynamic_index_in_dim(table, my_place, 0, keepdims=False)
    sources = my_ids // BLOCKS_DEV
    my_targets = lax.dynamic_slice_in_dim(group_map, my_place * BLOCKS_DEV, BLOCKS_DEV)
    first_block = jnp.zeros((), jnp.int32)
    one, other, live = tile_lists(group_lists[0], first_block, total_strips)

    row_place = (my_place * row_dev + jnp.arange(row_dev, dtype=jnp.int32)).astype(jnp.float32)
    col_place = (group_place * col_dev + jnp.arange(col_dev, dtype=jnp.int32)).astype(jnp.float32)
    location = jnp.stack(
        [row_place[:, None] + jitter[0], col_place[None, :] + jitter[1]], axis=0
    ).reshape(2, BLOCKS_DEV, STRIP, col_dev)
    location = location.transpose(1, 0, 2, 3).reshape(BLOCKS_DEV, 2 * STRIP, col_dev)
    before, after = beside(location, REACH)
    wider = jnp.concatenate([before, location, after], axis=0) * (1.0 / CUTOFF)
    hi_tiles, lo_tiles = covariance_tiles(one, other, live, wider, wider.transpose(0, 2, 1))

    weight = observed.astype(jnp.float32)
    spread_scale = huber_scale[:, None, None]
    row_effect = jnp.zeros((fields, row_dev), jnp.float32)
    col_effect = jnp.zeros((fields, col_dev), jnp.float32)
    row_count = jnp.ones((row_dev,), jnp.float32)
    col_count = jnp.ones((col_dev,), jnp.float32)
    for sweep_number in range(SWEEPS):
        clipped = jnp.clip(
            (observations - row_effect[:, :, None] - col_effect[:, None, :]) / spread_scale,
            -HUBER_EDGE,
            HUBER_EDGE,
        )
        row_part = jnp.sum(weight[None] * clipped, axis=2)
        if sweep_number == 0:
            row_part, row_total = sum_rows((row_part, jnp.sum(weight, axis=1)))
            row_count = jnp.maximum(row_total, 1.0)
        else:
            row_part = sum_rows(row_part)
        row_effect = row_effect + huber_scale[:, None] * row_part / row_count[None, :]
        clipped = jnp.clip(
            (observations - row_effect[:, :, None] - col_effect[:, None, :]) / spread_scale,
            -HUBER_EDGE,
            HUBER_EDGE,
        )
        col_part = jnp.sum(weight[None] * clipped, axis=1)
        if sweep_number == 0:
            col_part, col_total = sum_columns((col_part, jnp.sum(weight, axis=0)))
            col_count = jnp.maximum(col_total, 1.0)
        else:
            col_part = sum_columns(col_part)
        col_effect = col_effect + huber_scale[:, None] * col_part / col_count[None, :]
    residual_field = weight[None] * (observations - row_effect[:, :, None] - col_effect[:, None, :])
    r0 = residual_field.reshape(fields, BLOCKS_DEV, BLOCK).transpose(1, 0, 2)

    def apply_tiles(v):
        before, after = beside(v, REACH)
        part = own_product(one, other, live, v, hi_tiles, lo_tiles)
        return halo_product(one, other, live, before, after, part, hi_tiles, lo_tiles)

    m1 = apply_tiles(r0)
    owned_r0 = to_owners(r0, my_targets)
    m2 = apply_tiles(m1)
    owned_m1 = to_owners(m1, my_targets)
    dots = jnp.stack([jnp.sum(p * q, axis=(0, 2)) for p, q in ((r0, r0), (r0, m1), (m1, m1), (m1, m2))])
    owned_m2 = to_owners(m2, my_targets)
    dots = over_copies(over_copies(dots, WIDE), SIXTEEN)
    scale = step_scales(*dots)
    solution_now, residual_now = combined(sources, scale, owned_r0, owned_m1, owned_m2)
    return (solution_now[None, None], residual_now[None, None])


def solution(mesh):
    finer = Mesh(mesh.devices.reshape(4, 2, 4, 4), ("wide_0", "wide_1", "sixteen_0", "sixteen_1"))
    in_specs = (
        P(None, SIXTEEN, WIDE),
        P(),
        P(SIXTEEN, WIDE),
        P(None, SIXTEEN, WIDE),
        P(WIDE, None),
        P(WIDE, None, None),
    )
    out_specs = (P(WIDE, SIXTEEN, None, None, None), P(WIDE, SIXTEEN, None, None, None))
    return jax.shard_map(
        on_device, mesh=finer, in_specs=in_specs, out_specs=out_specs, check_vma=False
    )
```

time: 548 us -> 356 us (0.65)
  Pallas kernels: 0 us -> 137 us
  matrix products: 120 us -> 0 us
  other arithmetic: 110 us -> 14.7 us
  blocking collectives: 59.4 us -> 0 us
  local copies, waits for them, and re-layouts: 66 us -> 18.2 us
  loops' own time: 45.7 us -> 0 us
  waiting for transfers between devices: 87 us -> 114 us
  starting transfers between devices: 55.2 us -> 64.7 us
    pallas_call x0 -> x9, Pallas kernels: none -> 137 us  [the longest x2 47.6 us: own_product(): pl.pallas_call(own_kernel, grid_spec=pltpu.PrefetchScalarGridSpec(num_sca...]
    dot_general x20 -> x0, matrix products: 120 us -> none  [the longest x16 114 us: one_block(): jnp.einsum('fmb,mba->fa', stacked, kernel, precision=EXACT)]
    dynamic_update_slice x8 -> x0, other arithmetic: 65.8 us -> none  [on_device(): stored_tiles = lax.map(tiles_of, block_numbers)]
    psum x8 -> x0, blocking collectives: 59.4 us -> none  [one_axis_at_a_time(): return functools.reduce(lax.psum, axes, shard)]
    another operation x3 -> x0, loops' own time: 45.7 us -> none  [the longest x2 29.2 us: apply_operator(): return jnp.moveaxis(lax.map(one_block, block_numbers), 0, 1)]
    all_to_all x4 -> x3, waiting for transfers between devices: 41.7 us -> 76.4 us  [to_owners(): return lax.all_to_all(slots, SIXTEEN, 0, 0, tiled=True)]
    squeeze x16 -> x0, local copies, waits for them, and re-layouts: 19.1 us -> none  [one_block(): lax.dynamic_index_in_dim(near_values, position, 1, keepdims=False)]
    dynamic_slice x59 -> x1, local copies, waits for them, and re-layouts: 14.8 us -> 0.65 us  [on_device(): lax.dynamic_slice_in_dim(group_map, my_place * BLOCKS_DEV, BLOCKS_DEV)]
  transfers between devices with their start and end apart: 16 -> 17, of which waited for: 11 -> 11; matrix products, arithmetic and copies ran while one was open for 19% -> 7% of each run, Pallas kernels for 0% -> 29%
where the time goes in v1:
time: 356 us; the launch traced here: 352 us
  Pallas kernels  137 us (38%)
  waiting for transfers between devices  114 us (32%)
  starting transfers between devices  64.7 us (18%)
  local copies, waits for them, and re-layouts  18.2 us (5%)
  other arithmetic  14.7 us (4%)
    all_to_all x3, waiting for transfers between devices, to_owners(): return lax.all_to_all(slots, SIXTEEN, 0, 0, tiled=True)  76.4 us
    pallas_call x2, Pallas kernels, own_product(): pl.pallas_call(own_kernel, grid_spec=pltpu.PrefetchScalarGridSpec(num_sca...  47.6 us
    all_to_all x8, waiting for transfers between devices, sent_to_all(): lax.all_to_all(jnp.broadcast_to(shard[None], (peers, *shard.shape)), axis...  38.1 us
    pallas_call x1, Pallas kernels, covariance_tiles(): pl.pallas_call(tiles_kernel, grid_spec=pltpu.PrefetchScalarGridSpec(num_s...  35.8 us
    all_to_all x8, starting transfers between devices, sent_to_all(): lax.all_to_all(jnp.broadcast_to(shard[None], (peers, *shard.shape)), axis...  33.6 us
    pallas_call x2, Pallas kernels, halo_product(): pl.pallas_call(halo_kernel, grid_spec=pltpu.PrefetchScalarGridSpec(num_sc...  29.2 us
    pallas_call x3, Pallas kernels, to_owners(): pl.pallas_call(spread_kernel, grid_spec=pltpu.PrefetchScalarGridSpec(num_...  17.5 us
    all_to_all x3, starting transfers between devices, to_owners(): return lax.all_to_all(slots, SIXTEEN, 0, 0, tiled=True)  15 us
  transfers between devices with their start and end apart: 17, of which 11 were waited for; matrix products, arithmetic and copies ran while one was open for 7% of the time, Pallas kernels for 29%

profile of v1, /device:TPU:0, one launch (start us, length us, event | category | flops | bytes accessed | tf_op | source)
XLA Modules:
  0.0 352.0 jit_solution(16723020004856081936)
XLA Ops:
  2.2 4.6 %all-to-all-start.1 = ((f32[8,1,32]{2,1,0:T(1,128)}), f32[8,1,32]{2,1,0:T(1,128)S(1)}, u32[]{:S(2)}, u32[]{:S(2)}) async-start(f32[8,1,32]{2,1,0:T(1,128)} %broadcast_in_dim.45), calls=%async_computation.1 | async-start | bytes 8192 | tf_op jit(solution)/shard_map/all_to_all | solution.py:36
  15.8 5.6 %all-to-all-done = f32[8,1,2048]{2,1,0:T(1,128)S(1)} async-done(((f32[8,1,2048]{2,1,0:T(1,128)}), f32[8,1,2048]{2,1,0:T(1,128)S(1)}, u32[]{:S(2)}, u32[]{:S(2)}) %all-to-all-start) | async-done | bytes 65568 | tf_op jit(solution)/shard_map/all_to_all | solution.py:36
  22.0 7.9 %all-to-all-start.3 = ((f32[16,1,128]{2,1,0:T(1,128)}), f32[16,1,128]{2,1,0:T(1,128)S(1)}, u32[]{:S(2)}, u32[]{:S(2)}) async-start(f32[16,1,128]{2,1,0:T(1,128)} %broadcast_in_dim.47), calls=%async_computation.3 | async-start | bytes 16384 | tf_op jit(solution)/shard_map/all_to_all | solution.py:36
  32.0 5.3 %all-to-all-done.3 = f32[16,1,128]{2,1,0:T(1,128)S(1)} async-done(((f32[16,1,128]{2,1,0:T(1,128)}), f32[16,1,128]{2,1,0:T(1,128)S(1)}, u32[]{:S(2)}, u32[]{:S(2)}) %all-to-all-start.3) | async-done | bytes 8224 | tf_op jit(solution)/shard_map/all_to_all | solution.py:36
  49.1 5.6 %all-to-all-done.2 = f32[16,64,128]{2,1,0:T(8,128)S(1)} async-done(((f32[16,64,128]{2,1,0:T(8,128)}), f32[16,64,128]{2,1,0:T(8,128)S(1)}, u32[]{:S(2)}, u32[]{:S(2)}) %all-to-all-start.2) | async-done | bytes 524320 | tf_op jit(solution)/shard_map/all_to_all | solution.py:36
  60.0 5.4 %all-to-all-done.4 = f32[8,1,2048]{2,1,0:T(1,128)S(1)} async-done(((f32[8,1,2048]{2,1,0:T(1,128)}), f32[8,1,2048]{2,1,0:T(1,128)S(1)}, u32[]{:S(2)}, u32[]{:S(2)}) %all-to-all-start.4) | async-done | bytes 65568 | tf_op jit(solution)/shard_map/all_to_all | solution.py:36
  74.2 8.8 %all-to-all-done.5 = f32[16,64,128]{2,1,0:T(8,128)S(1)} async-done(((f32[16,64,128]{2,1,0:T(8,128)}), f32[16,64,128]{2,1,0:T(8,128)S(1)}, u32[]{:S(2)}, u32[]{:S(2)}) %all-to-all-start.5) | async-done | bytes 524320 | tf_op jit(solution)/shard_map/all_to_all | solution.py:36
  86.1 4.8 %collective-permute-start.1 = (f32[4,64,512]{2,1,0:T(8,128)}, f32[4,64,512]{2,1,0:T(8,128)S(1)}, u32[]{:S(2)}, u32[]{:S(2)}) collective-permute-start(f32[4,64,512]{2,1,0:T(8,128)} %get-tuple-element.30), channel_id=1, source_target_pairs={{1,0},{2,1},{3,2},{4,3},{5,4},{6,5},{7,6},{8,7},{9,8},{10,9},{11,1... | collective-permute-start | bytes 1572872 | tf_op jit(solution)/shard_map/ppermute | solution.py:50
  95.9 35.8 %tiles.1 = (bf16[44,512,512]{2,1,0:T(8,128)(2,1)}, bf16[44,512,512]{2,1,0:T(8,128)(2,1)}) custom-call(s32[44]{0:T(128)S(1)} %get-tuple-element.40.a_ref, s32[44]{0:T(128)S(1)} %get-tuple-element.39.b_ref, s32[44]{0:T(128)S(1)} %add_convert_fusion.live_ref, f32[16,8,128]{2,1,0:T(8,128)S(1)} %copy.99.rows_ref, f32[16,128,8]{2,1,0:T(8,128)S(1)} %get-tuple-element.28.cols_ref), custom_call_target="tpu_custom_call" | custom-call | tf_op jit(solution)/shard_map/tiles/pallas_call | solution.py:148
  131.8 23.8 %own.2.part_ref = f32[8,64,512]{2,1,0:T(8,128)S(1)} custom-call(s32[44]{0:T(128)S(1)} %get-tuple-element.40.a_ref, s32[44]{0:T(128)S(1)} %get-tuple-element.39.b_ref, s32[44]{0:T(128)S(1)} %add_convert_fusion.live_ref, f32[8,64,512]{2,1,0:T(8,128)S(1)} %bitcast.87, bf16[44,512,512]{2,1,0:T(8,128)(2,1)} %get-tuple-element.6.hi_ref, ...), custom_call_target="tpu_custom_call" | custom-call | tf_op jit(solution)/shard_map/own/pallas_call | solution.py:227
  159.2 14.6 %halo.2.v_ref = f32[8,64,512]{2,1,0:T(8,128)S(1)} custom-call(s32[44]{0:T(128)S(1)} %get-tuple-element.40.a_ref, s32[44]{0:T(128)S(1)} %get-tuple-element.39.b_ref, s32[44]{0:T(128)S(1)} %add_convert_fusion.live_ref, f32[4,64,512]{2,1,0:T(8,128)S(1)} %copy-done.4, f32[4,64,512]{2,1,0:T(8,128)S(1)} %copy-done.6, f32[8,64,512]{2,1,0:T(8,128)S(1)} %own.2.part_ref, ...), custom_call_target="tpu_custom_call" | custom-call | tf_op jit(solution)/shard_map/halo/pallas_call | solution.py:246
  174.0 5.3 %collective-permute-start.5 = (f32[4,64,512]{2,1,0:T(8,128)S(1)}, f32[4,64,512]{2,1,0:T(8,128)S(1)}, u32[]{:S(2)}, u32[]{:S(2)}) collective-permute-start(f32[4,64,512]{2,1,0:T(8,128)S(1)} %get-tuple-element.26), channel_id=1, source_target_pairs={{1,0},{2,1},{3,2},{4,3},{5,4},{6,5},{7,6},{8,7},{9,8},{10,9},{11,1... | collective-permute-start | bytes 1572872 | tf_op jit(solution)/shard_map/ppermute | solution.py:50
  179.3 23.8 %own.3.part_ref = f32[8,64,512]{2,1,0:T(8,128)S(1)} custom-call(s32[44]{0:T(128)S(1)} %get-tuple-element.40.a_ref, s32[44]{0:T(128)S(1)} %get-tuple-element.39.b_ref, s32[44]{0:T(128)S(1)} %add_convert_fusion.live_ref, f32[8,64,512]{2,1,0:T(8,128)S(1)} %halo.2.v_ref, bf16[44,512,512]{2,1,0:T(8,128)(2,1)} %get-tuple-element.6.hi_ref, ...), custom_call_target="tpu_custom_call" | custom-call | tf_op jit(solution)/shard_map/own/pallas_call | solution.py:227
  203.1 14.6 %halo.3.v_ref = f32[8,64,512]{2,1,0:T(8,128)S(1)} custom-call(s32[44]{0:T(128)S(1)} %get-tuple-element.40.a_ref, s32[44]{0:T(128)S(1)} %get-tuple-element.39.b_ref, s32[44]{0:T(128)S(1)} %add_convert_fusion.live_ref, f32[4,64,512]{2,1,0:T(8,128)S(1)} %collective-permute-done.4.before_ref, f32[4,64,512]{2,1,0:T(8,128)S(1)} %collective-permute-done.5.after_ref, ...), custom_call_target="tpu_custom_call" | custom-call | tf_op jit(solution)/shard_map/halo/pallas_call | solution.py:246
  222.8 5.2 %all-to-all-done.6 = f32[8,1,256]{2,1,0:T(1,128)S(1)} async-done(((f32[8,1,256]{2,1,0:T(1,128)}), f32[8,1,256]{2,1,0:T(1,128)S(1)}, u32[]{:S(2)}, u32[]{:S(2)}) %all-to-all-start.6) | async-done | bytes 8224 | tf_op jit(solution)/shard_map/all_to_all | solution.py:36
  233.7 5.9 %spread.3 = f32[16,64,512]{2,1,0:T(8,128)} custom-call(s32[8]{0:T(128)} %dynamic-slice_bitcast_fusion.slot_ref, f32[8,64,512]{2,1,0:T(8,128)} %bitcast.88), custom_call_target="tpu_custom_call" | custom-call | tf_op jit(solution)/shard_map/spread/pallas_call | solution.py:314
  240.5 6.1 %all-to-all-start.8 = ((f32[16,64,512]{2,1,0:T(8,128)}), f32[16,64,512]{2,1,0:T(8,128)S(1)}, u32[]{:S(2)}, u32[]{:S(2)}) async-start(f32[16,64,512]{2,1,0:T(8,128)} %spread.3), calls=%async_computation.8 | async-start | bytes 4194304 | tf_op jit(solution)/shard_map/all_to_all | solution.py:325
  246.7 5.8 %spread.4 = f32[16,64,512]{2,1,0:T(8,128)} custom-call(s32[8]{0:T(128)} %dynamic-slice_bitcast_fusion.slot_ref, f32[8,64,512]{2,1,0:T(8,128)} %copy-done), custom_call_target="tpu_custom_call" | custom-call | tf_op jit(solution)/shard_map/spread/pallas_call | solution.py:314
  252.5 25.0 %all-to-all-done.8.refs_0_.refs_3_.refs_6_.refs_9_.refs_12_.refs_15_.refs_18_.refs_21_ = f32[16,64,512]{2,1,0:T(8,128)S(1)} async-done(((f32[16,64,512]{2,1,0:T(8,128)}), f32[16,64,512]{2,1,0:T(8,128)S(1)}, u32[]{:S(2)}, u32[]{:S(2)}) %all-to-all-start.8) | async-done | bytes 2097184 | tf_op jit(solution)/shard_map/all_to_all | solution.py:325
  282.0 5.8 %spread.5 = f32[16,64,512]{2,1,0:T(8,128)} custom-call(s32[8]{0:T(128)} %dynamic-slice_bitcast_fusion.slot_ref, f32[8,64,512]{2,1,0:T(8,128)} %copy-done.2), custom_call_target="tpu_custom_call" | custom-call | tf_op jit(solution)/shard_map/spread/pallas_call | solution.py:314
  287.8 23.7 %all-to-all-done.9.refs_1_.refs_4_.refs_7_.refs_10_.refs_13_.refs_16_.refs_19_.refs_22_ = f32[16,64,512]{2,1,0:T(8,128)} async-done(((f32[16,64,512]{2,1,0:T(8,128)}), f32[16,64,512]{2,1,0:T(8,128)}, u32[]{:S(2)}, u32[]{:S(2)}) %all-to-all-start.9) | async-done | bytes 2097184 | tf_op jit(solution)/shard_map/all_to_all | solution.py:325
  311.5 4.4 %all-to-all-start.10 = ((f32[16,64,512]{2,1,0:T(8,128)}), f32[16,64,512]{2,1,0:T(8,128)}, u32[]{:S(2)}, u32[]{:S(2)}) async-start(f32[16,64,512]{2,1,0:T(8,128)} %spread.5), calls=%async_computation.10 | async-start | bytes 4194304 | tf_op jit(solution)/shard_map/all_to_all | solution.py:325
  317.7 27.6 %all-to-all-done.10.refs_2_.refs_5_.refs_8_.refs_11_.refs_14_.refs_17_.refs_20_.refs_23_ = f32[16,64,512]{2,1,0:T(8,128)} async-done(((f32[16,64,512]{2,1,0:T(8,128)}), f32[16,64,512]{2,1,0:T(8,128)}, u32[]{:S(2)}, u32[]{:S(2)}) %all-to-all-start.10) | async-done | bytes 2097184 | tf_op jit(solution)/shard_map/all_to_all | solution.py:325
  345.3 6.6 %combine.1 = (f32[64,8,512]{2,1,0:T(8,128)}, f32[64,8,512]{2,1,0:T(8,128)}) custom-call(s32[8]{0:T(128)S(1)} %and_select_fusion.1.src_ref, f32[64,8]{1,0:T(8,128)S(1)} %copy.102.scale_ref, f32[16,64,512]{2,1,0:T(8,128)S(1)} %all-to-all-done.8.refs_0_.refs_3_.refs_6_.refs_9_.refs_12_.refs_15_.refs_18_.refs_21_, ...), custom_call_target="tpu_custom_call" | custom-call | tf_op jit(solution)/shard_map/combine/pallas_call | solution.py:292
  (137 shorter events, 66.6 us)
Async XLA Ops:
  0.6 30.9 %copy-start.7 = (f32[64,32,128]{2,1,0:T(8,128)S(1)}, f32[64,32,128]{2,1,0:T(8,128)}, u32[]{:S(2)}) copy-start(f32[64,32,128]{2,1,0:T(8,128)} %param.6) | copy-start | bytes 3145732
  0.6 30.7 %copy-start.10 = (f32[64]{0:T(128)S(1)}, f32[64]{0:T(128)}, u32[]{:S(2)}) copy-start(f32[64]{0:T(128)} %param.7) | copy-start | bytes 772
  2.2 9.7 %all-to-all-start.1 = ((f32[8,1,32]{2,1,0:T(1,128)}), f32[8,1,32]{2,1,0:T(1,128)S(1)}, u32[]{:S(2)}, u32[]{:S(2)}) async-start(f32[8,1,32]{2,1,0:T(1,128)} %broadcast_in_dim.45), calls=%async_computation.1 | async-start | bytes 8192 | tf_op jit(solution)/shard_map/all_to_all | solution.py:36
  10.8 38.0 %copy-start.11 = (s32[1,128,6]{1,0,2:T(1,128)S(1)}, s32[1,128,6]{1,0,2:T(1,128)}, u32[]{:S(2)}) copy-start(s32[1,128,6]{1,0,2:T(1,128)} %param.11) | copy-start | bytes 9220
  11.9 9.4 %all-to-all-start = ((f32[8,1,2048]{2,1,0:T(1,128)}), f32[8,1,2048]{2,1,0:T(1,128)S(1)}, u32[]{:S(2)}, u32[]{:S(2)}) async-start(f32[8,1,2048]{2,1,0:T(1,128)} %reshape.577), calls=%async_computation | async-start | bytes 131072 | tf_op jit(solution)/shard_map/all_to_all | solution.py:36
  22.0 15.4 %all-to-all-start.3 = ((f32[16,1,128]{2,1,0:T(1,128)}), f32[16,1,128]{2,1,0:T(1,128)S(1)}, u32[]{:S(2)}, u32[]{:S(2)}) async-start(f32[16,1,128]{2,1,0:T(1,128)} %broadcast_in_dim.47), calls=%async_computation.3 | async-start | bytes 16384 | tf_op jit(solution)/shard_map/all_to_all | solution.py:36
  38.2 16.5 %all-to-all-start.2 = ((f32[16,64,128]{2,1,0:T(8,128)}), f32[16,64,128]{2,1,0:T(8,128)S(1)}, u32[]{:S(2)}, u32[]{:S(2)}) async-start(f32[16,64,128]{2,1,0:T(8,128)} %broadcast_in_dim.46), calls=%async_computation.2 | async-start | bytes 1048576 | tf_op jit(solution)/shard_map/all_to_all | solution.py:36
  42.6 49.5 %collective-permute-start.2 = (f32[4,8,128]{1,2,0:T(8,128)}, f32[4,8,128]{1,2,0:T(8,128)S(1)}, u32[]{:S(2)}, u32[]{:S(2)}) collective-permute-start(f32[4,8,128]{1,2,0:T(8,128)} %copy.94), channel_id=1, source_target_pairs={{0,1},{1,2},{2,3},{3,4},{4,5},{5,6},{6,7},{7,8},{8,9},{9,10},{10,1... | collective-permute-start | bytes 49160 | tf_op jit(solution)/shard_map/ppermute | solution.py:49
  45.3 46.9 %collective-permute-start.3 = (f32[4,8,128]{1,2,0:T(8,128)}, f32[4,8,128]{1,2,0:T(8,128)}, u32[]{:S(2)}, u32[]{:S(2)}) collective-permute-start(f32[4,8,128]{1,2,0:T(8,128)} %copy.97), channel_id=1, source_target_pairs={{1,0},{2,1},{3,2},{4,3},{5,4},{6,5},{7,6},{8,7},{9,8},{10,9},{11,1... | collective-permute-start | bytes 49160 | tf_op jit(solution)/shard_map/ppermute | solution.py:50
  56.4 8.9 %all-to-all-start.4 = ((f32[8,1,2048]{2,1,0:T(1,128)}), f32[8,1,2048]{2,1,0:T(1,128)S(1)}, u32[]{:S(2)}, u32[]{:S(2)}) async-start(f32[8,1,2048]{2,1,0:T(1,128)} %reshape.579), calls=%async_computation.4 | async-start | bytes 131072 | tf_op jit(solution)/shard_map/all_to_all | solution.py:36
  67.8 15.3 %all-to-all-start.5 = ((f32[16,64,128]{2,1,0:T(8,128)}), f32[16,64,128]{2,1,0:T(8,128)S(1)}, u32[]{:S(2)}, u32[]{:S(2)}) async-start(f32[16,64,128]{2,1,0:T(8,128)} %broadcast_in_dim.49), calls=%async_computation.5 | async-start | bytes 1048576 | tf_op jit(solution)/shard_map/all_to_all | solution.py:36
  84.3 47.5 %copy-start.1 = (f32[64,8,512]{2,0,1:T(8,128)}, f32[64,8,512]{2,0,1:T(8,128)S(1)}, u32[]{:S(2)}) copy-start(f32[64,8,512]{2,0,1:T(8,128)S(1)} %copy.114) | copy-start | bytes 3145732
  85.5 70.0 %collective-permute-start = (f32[4,64,512]{2,1,0:T(8,128)}, f32[4,64,512]{2,1,0:T(8,128)S(1)}, u32[]{:S(2)}, u32[]{:S(2)}) collective-permute-start(f32[4,64,512]{2,1,0:T(8,128)} %get-tuple-element.31), channel_id=1, source_target_pairs={{0,1},{1,2},{2,3},{3,4},{4,5},{5,6},{6,7},{7,8},{8,9},{9,10},{10,1... | collective-permute-start | bytes 1572872 | tf_op jit(solution)/shard_map/ppermute | solution.py:49
  86.1 70.2 %collective-permute-start.1 = (f32[4,64,512]{2,1,0:T(8,128)}, f32[4,64,512]{2,1,0:T(8,128)S(1)}, u32[]{:S(2)}, u32[]{:S(2)}) collective-permute-start(f32[4,64,512]{2,1,0:T(8,128)} %get-tuple-element.30), channel_id=1, source_target_pairs={{1,0},{2,1},{3,2},{4,3},{5,4},{6,5},{7,6},{8,7},{9,8},{10,9},{11,1... | collective-permute-start | bytes 1572872 | tf_op jit(solution)/shard_map/ppermute | solution.py:50
  173.9 43.9 %copy-start = (f32[8,64,512]{2,1,0:T(8,128)}, f32[8,64,512]{2,1,0:T(8,128)S(1)}, u32[]{:S(2)}) copy-start(f32[8,64,512]{2,1,0:T(8,128)S(1)} %halo.2.v_ref) | copy-start | bytes 3145732
  173.9 29.2 %collective-permute-start.4 = (f32[4,64,512]{2,1,0:T(8,128)S(1)}, f32[4,64,512]{2,1,0:T(8,128)S(1)}, u32[]{:S(2)}, u32[]{:S(2)}) collective-permute-start(f32[4,64,512]{2,1,0:T(8,128)S(1)} %get-tuple-element.27), channel_id=1, source_target_pairs={{0,1},{1,2},{2,3},{3,4},{4,5},{5,6},{6,7},{7,8},{8,9},{9,10},{10,1... | collective-permute-start | bytes 1572872 | tf_op jit(solution)/shard_map/ppermute | solution.py:49
  174.0 29.1 %collective-permute-start.5 = (f32[4,64,512]{2,1,0:T(8,128)S(1)}, f32[4,64,512]{2,1,0:T(8,128)S(1)}, u32[]{:S(2)}, u32[]{:S(2)}) collective-permute-start(f32[4,64,512]{2,1,0:T(8,128)S(1)} %get-tuple-element.26), channel_id=1, source_target_pairs={{1,0},{2,1},{3,2},{4,3},{5,4},{6,5},{7,6},{8,7},{9,8},{10,9},{11,1... | collective-permute-start | bytes 1572872 | tf_op jit(solution)/shard_map/ppermute | solution.py:50
  203.1 14.6 %copy-start.9 = (f32[64,8,512]{2,1,0:T(8,128)S(1)}, f32[64,8,512]{2,1,0:T(8,128)}, u32[]{:S(2)}) copy-start(f32[64,8,512]{2,1,0:T(8,128)} %copy-done.8) | copy-start | bytes 3145732
  217.8 15.3 %copy-start.12 = (s32[1,128]{1,0:T(1,128)S(1)}, s32[1,128]{1,0:T(1,128)}, u32[]{:S(2)}) copy-start(s32[1,128]{1,0:T(1,128)} %param.10) | copy-start | bytes 1540
  219.4 8.6 %all-to-all-start.6 = ((f32[8,1,256]{2,1,0:T(1,128)}), f32[8,1,256]{2,1,0:T(1,128)S(1)}, u32[]{:S(2)}, u32[]{:S(2)}) async-start(f32[8,1,256]{2,1,0:T(1,128)} %reshape.581), calls=%async_computation.6 | async-start | bytes 16384 | tf_op jit(solution)/shard_map/all_to_all | solution.py:36
  229.5 11.0 %all-to-all-start.7 = ((f32[16,1,256]{2,1,0:T(1,128)}), f32[16,1,256]{2,1,0:T(1,128)S(1)}, u32[]{:S(2)}, u32[]{:S(2)}) async-start(f32[16,1,256]{2,1,0:T(1,128)} %reshape.583), calls=%async_computation.7 | async-start | bytes 32768 | tf_op jit(solution)/shard_map/all_to_all | solution.py:36
  240.5 37.0 %all-to-all-start.8 = ((f32[16,64,512]{2,1,0:T(8,128)}), f32[16,64,512]{2,1,0:T(8,128)S(1)}, u32[]{:S(2)}, u32[]{:S(2)}) async-start(f32[16,64,512]{2,1,0:T(8,128)} %spread.3), calls=%async_computation.8 | async-start | bytes 4194304 | tf_op jit(solution)/shard_map/all_to_all | solution.py:325
  277.5 34.0 %all-to-all-start.9 = ((f32[16,64,512]{2,1,0:T(8,128)}), f32[16,64,512]{2,1,0:T(8,128)}, u32[]{:S(2)}, u32[]{:S(2)}) async-start(f32[16,64,512]{2,1,0:T(8,128)} %spread.4), calls=%async_computation.9 | async-start | bytes 4194304 | tf_op jit(solution)/shard_map/all_to_all | solution.py:325
  311.5 33.8 %all-to-all-start.10 = ((f32[16,64,512]{2,1,0:T(8,128)}), f32[16,64,512]{2,1,0:T(8,128)}, u32[]{:S(2)}, u32[]{:S(2)}) async-start(f32[16,64,512]{2,1,0:T(8,128)} %spread.5), calls=%async_computation.10 | async-start | bytes 4194304 | tf_op jit(solution)/shard_map/all_to_all | solution.py:325
  (6 other events, 6.5 us)
